TPU v7x, 128 devices: a whole 4x4x4 slice. The times are simulated.
128 devices in a mesh: tile: 32 (over x, z, core), cuts: 4 (over y).
Axes of the slice: x: 4, y: 4, z: 4, core: 2. Of those that a mesh axis runs over, the one named last changes fastest.
Arguments:
- amplitudes: float32 [1024, 128, 128], P(('tile', 'cuts')), may hold values from 0 to 2
- positions: int32 [1024, 2], replicated, may hold values from 0 to 3968, as said below
- probe_field: float32 [2, 128, 128], replicated, may hold values from -4 to 4
- object_slices: float32 [4, 2, 256, 4096], P('cuts', None, None, 'tile'), may hold values from -1 to 1, as said below
Outputs:
- refined_object: float32 [4, 2, 256, 4096], P('cuts', None, None, 'tile')
Inputs may be any that keep to these rules, and one draw needn't show every extreme that they name: `positions`: rows lie in 0 .. 128; every frame's 128 columns lie inside the 4096 columns. A frame's owner tile is its column // 128. Frames are read in blocks of 8 consecutive frames, one block per device of tile+cuts in mesh order; one block holds at most 2 frames of any owner tile, and some block holds exactly 2. For every cuts index, the blocks of that index hold at most 16 frames of any one owner tile, and in every draw some owner tile receives exactly 16 from them. `object_slices`: transmissions have modulus at most 1.
All inputs are finite; a program needn't handle non-finite values.
Results may differ from a plain program's by a relative error of at most 0.015.
Values may be sent and summed in bfloat16 or wider, within the bound.
A program may use at most 128 MiB of HBM per device.

v0:
```python
import math
import jax
import jax.numpy as jnp
from jax import lax
from jax.sharding import PartitionSpec as P

ITERS = 2
STEP_SIZE = 0.05
AMPLITUDE_FLOOR = 0.25


def passed_along(x, axis, by):
    peers = lax.axis_size(axis)
    pairs = [(i, i + by) for i in range(peers) if 0 <= i + by < peers]
    return lax.ppermute(x, axis, pairs)


def block_table(real_part, imag_part):
    upper = jnp.stack([real_part, imag_part], axis=1)
    lower = jnp.stack([-imag_part, real_part], axis=1)
    return jnp.stack([upper, lower], axis=0).astype(jnp.bfloat16)


def make_tables(frame_side):
    highest = lax.Precision.HIGHEST
    index = jnp.arange(frame_side, dtype=jnp.int32)
    product = index[:, None] * index[None, :] % frame_side
    angle = product.astype(jnp.float32) * (2.0 * math.pi / frame_side)
    norm_scale = 1.0 / math.sqrt(frame_side)
    four_real = jnp.cos(angle) * norm_scale
    four_imag = -jnp.sin(angle) * norm_scale
    centred = (index + frame_side // 2) % frame_side - frame_side // 2
    chirp = -math.pi * (centred * centred).astype(jnp.float32) / (4.0 * frame_side)
    chirp_real = jnp.cos(chirp)
    chirp_imag = jnp.sin(chirp)
    left_real = four_real * chirp_real[None, :] + four_imag * chirp_imag[None, :]
    left_imag = four_real * chirp_imag[None, :] - four_imag * chirp_real[None, :]
    prop_real = jnp.dot(left_real, four_real, precision=highest) - jnp.dot(
        left_imag, four_imag, precision=highest
    )
    prop_imag = jnp.dot(left_real, four_imag, precision=highest) + jnp.dot(
        left_imag, four_real, precision=highest
    )
    return (
        block_table(four_real, four_imag),
        block_table(four_real, -four_imag),
        block_table(prop_real, prop_imag),
        block_table(prop_real, -prop_imag),
    )


def right_product(field, table):
    return jnp.einsum(
        "fcij,cjdk->fdik", field.astype(jnp.bfloat16), table, preferred_element_type=jnp.float32
    )


def two_sided(field, table):
    first = right_product(field, table)
    second = right_product(jnp.swapaxes(first, -1, -2), table)
    return jnp.swapaxes(second, -1, -2)


def complex_times(left, right):
    real_part = left[..., 0, :, :] * right[..., 0, :, :] - left[..., 1, :, :] * right[..., 1, :, :]
    imag_part = left[..., 0, :, :] * right[..., 1, :, :] + left[..., 1, :, :] * right[..., 0, :, :]
    return jnp.stack([real_part, imag_part], axis=-3)


def conj_times(left, right):
    real_part = left[..., 0, :, :] * right[..., 0, :, :] + left[..., 1, :, :] * right[..., 1, :, :]
    imag_part = left[..., 0, :, :] * right[..., 1, :, :] - left[..., 1, :, :] * right[..., 0, :, :]
    return jnp.stack([real_part, imag_part], axis=-3)


def frame_patches(windows, probe_field, measured, tables):
    four, four_conj, prop, prop_conj = tables
    slice_count = windows.shape[1]
    wave = complex_times(probe_field[None], windows[:, 0].astype(jnp.float32))
    fields = []
    for level in range(1, slice_count):
        moved = two_sided(wave, prop)
        fields.append(moved)
        wave = complex_times(windows[:, level].astype(jnp.float32), moved)
    far = two_sided(wave, four)
    magnitude = jnp.sqrt(far[:, 0] * far[:, 0] + far[:, 1] * far[:, 1])
    factor = 1.0 - measured / jnp.maximum(magnitude, AMPLITUDE_FLOOR)
    back = two_sided(far * factor[:, None], four_conj)
    patches = [None] * slice_count
    for level in range(slice_count - 1, 0, -1):
        patches[level] = conj_times(fields[level - 1], back)
        back = two_sided(conj_times(windows[:, level].astype(jnp.float32), back), prop_conj)
    patches[0] = conj_times(probe_field[None], back)
    return jnp.stack(patches, axis=1)


def cut_windows(panel, frame_rows, frame_cols, frame_side):
    zero_index = jnp.zeros((), jnp.int32)

    def window_at(row_start, col_start):
        start = (zero_index, zero_index, row_start, col_start)
        return lax.dynamic_slice(
            panel, start, (panel.shape[0], panel.shape[1], frame_side, frame_side)
        )

    return jax.vmap(window_at)(frame_rows, frame_cols)


def place_patches(panel_shape, patches, frame_rows, frame_cols, weights):
    panel_height = panel_shape[-2]
    panel_width = panel_shape[-1]
    frame_side = patches.shape[-1]
    offsets = jnp.arange(frame_side, dtype=jnp.int32)
    col_target = frame_cols[:, None] + offsets[None, :]
    col_onehot = (
        col_target[:, :, None] == jnp.arange(panel_width, dtype=jnp.int32)[None, None, :]
    ).astype(jnp.bfloat16)
    row_target = frame_rows[:, None] + offsets[None, :]
    row_onehot = (
        jnp.arange(panel_height, dtype=jnp.int32)[:, None, None] == row_target[None, :, :]
    ).astype(jnp.bfloat16)
    remain = patches * weights[:, None, None, None, None]
    gathered_sum = jnp.zeros(panel_shape, jnp.float32)
    for piece_index in range(3):
        piece_part = remain.astype(jnp.bfloat16)
        remain = remain - piece_part.astype(jnp.float32)
        placed_cols = jnp.einsum(
            "fscij,fjk->fscik", piece_part, col_onehot, preferred_element_type=jnp.float32
        ).astype(jnp.bfloat16)
        gathered_sum = gathered_sum + jnp.einsum(
            "hfi,fscik->schk", row_onehot, placed_cols, preferred_element_type=jnp.float32
        )
    return gathered_sum


def reduce_gradient(term_part):
    return lax.psum_scatter(term_part, "cuts", scatter_dimension=0, tiled=True)


def add_rim(main_part, moved_rim):
    extra = main_part.shape[-1] - moved_rim.shape[-1]
    return main_part + moved_rim


def body(amplitudes, positions, probe_field, object_slices):
    tile_count = lax.axis_size("tile")
    cut_count = lax.axis_size("cuts")
    tile_id = lax.axis_index("tile")
    cut_id = lax.axis_index("cuts")
    frame_side = probe_field.shape[-1]
    frames_held = amplitudes.shape[0]
    tile_width = object_slices.shape[-1]
    total_frames = positions.shape[0]
    reader_count = total_frames // frames_held
    capacity = max(2, 2 * frames_held // tile_count)
    max_load = 2 * frames_held
    row_list = positions[:, 0]
    col_list = positions[:, 1]
    owner = col_list // tile_width
    owner_grid = owner.reshape(reader_count, frames_held)
    earlier = jnp.tril(jnp.ones((frames_held, frames_held), jnp.int32), -1)
    same_owner = (owner_grid[:, :, None] == owner_grid[:, None, :]).astype(jnp.int32)
    slot_grid = jnp.sum(same_owner * earlier[None], axis=2)
    slot_list = slot_grid.reshape(total_frames)
    reader_self = tile_id * cut_count + cut_id
    my_owner = lax.dynamic_index_in_dim(owner_grid, reader_self, 0, keepdims=False)
    my_slot = lax.dynamic_index_in_dim(slot_grid, reader_self, 0, keepdims=False)
    target = my_owner * capacity + my_slot
    source = (
        jnp.full((tile_count * capacity,), frames_held, jnp.int32)
        .at[target]
        .set(jnp.arange(frames_held, dtype=jnp.int32))
    )
    padded = jnp.concatenate(
        [amplitudes, jnp.zeros((1, frame_side, frame_side), amplitudes.dtype)], axis=0
    )
    outgoing = jnp.take(padded, source, axis=0).reshape(
        tile_count, capacity, frame_side, frame_side
    )
    incoming = lax.all_to_all(outgoing, "tile", split_axis=0, concat_axis=0, tiled=True)
    reader_of = jnp.arange(total_frames, dtype=jnp.int32) // frames_held
    mine = (owner == tile_id) & (reader_of % cut_count == cut_id)
    rank_list = jnp.cumsum(mine.astype(jnp.int32)) - 1
    spot_list = jnp.where(mine, rank_list, max_load)
    chosen = (
        jnp.zeros((max_load,), jnp.int32)
        .at[spot_list]
        .set(jnp.arange(total_frames, dtype=jnp.int32), mode="drop")
    )
    live_weight = jnp.zeros((max_load,), jnp.float32).at[spot_list].set(1.0, mode="drop")
    flat_slot = reader_of // cut_count * capacity + slot_list
    picked = jnp.take(flat_slot, chosen)
    frames_in = jnp.take(
        incoming.reshape(tile_count * capacity, frame_side, frame_side), picked, axis=0
    )
    frame_rows = jnp.take(row_list, chosen)
    frame_cols = jnp.take(col_list, chosen) - tile_id * tile_width
    tables = make_tables(frame_side)
    current = object_slices
    for turn in range(ITERS):
        stacked = lax.all_gather(current.astype(jnp.bfloat16), "cuts", axis=0, tiled=True)
        next_rim = passed_along(stacked, "tile", -1)
        panel = jnp.concatenate([stacked, next_rim], axis=-1)
        windows = cut_windows(panel, frame_rows, frame_cols, frame_side)
        patches = frame_patches(windows, probe_field, frames_in, tables)
        term = place_patches(panel.shape, patches, frame_rows, frame_cols, live_weight)
        moved = passed_along(term[..., tile_width:], "tile", 1)
        share = reduce_gradient(add_rim(term[..., :tile_width], moved))
        current = current - STEP_SIZE * share
    return current


def solution(mesh):
    in_specs = (P(("tile", "cuts"), None, None), P(), P(), P("cuts", None, None, "tile"))
    out_specs = P("cuts", None, None, "tile")
    return jax.shard_map(body, mesh=mesh, in_specs=in_specs, out_specs=out_specs, check_vma=False)
```

profile of v0, /device:TPU:0, one launch (start us, length us, event | category | flops | bytes accessed | tf_op | source)
XLA Modules:
  0.0 458.6 jit_solution(10593045391714817191)
XLA Ops:
  7.5 13.4 %all_gather.6 = bf16[4,2,256,128]{3,2,1,0:T(8,128)(2,1)S(1)} all-gather(bf16[1,2,256,128]{3,2,1,0:T(8,128)(2,1)S(1)} %convert_element_type.304), channel_id=1, replica_groups=mesh['tile'=32,'cuts'=4] {'cuts'}, dimensions={0}, use_global_device_ids=true | all-gather | bytes 655360 | tf_op jit(solution)/shard_map/all_gather | solution.py:201
  26.8 2.8 gather_fusion
  29.6 4.5 broadcast_select_fusion
  34.1 9.0 %all-to-all-start = ((f32[32,2,128,128]{3,2,1,0:T(8,128)}), f32[32,2,128,128]{3,2,1,0:T(8,128)}, u32[]{:S(2)}, u32[]{:S(2)}) async-start(f32[32,2,128,128]{3,2,1,0:T(8,128)} %broadcast_select_fusion), calls=%async_computation | async-start | bytes 8388608 | tf_op jit(solution)/shard_map/all_to_all | solution.py:180
  44.9 4.3 scatter_custom_fusion
  52.8 4.8 %scatter_custom_fusion.2 = f32[16]{0:T(128)} fusion(s32[1024]{0:T(1024)S(1)} %bitcast.768, f32[1024]{0:T(1024)S(1)} %broadcast.687, f32[]{:T(128)} %constant.180.clone.1), kind=kCustom, calls=%fused_computation.444 | custom fusion | bytes 68 | tf_op jit(solution)/shard_map/scatter | solution.py:190
  59.3 3.1 broadcast.645.clone2
  62.3 44.7 %while.2 = (s32[]{:T(128)}, bf16[4,2,256,256]{3,2,1,0:T(8,128)(2,1)S(1)}, s32[16,4]{0,1:T(4,128)S(1)}, bf16[16,4,2,128,128]{4,3,2,0,1:T(8,128)(2,1)}, s32[]{:T(128)}) while((s32[]{:T(128)}, bf16[4,2,256,256]{3,2,1,0:T(8,128)(2,1)S(1)}, s32[16,4]{0,1:T(4,128)S(1)}, bf16[16,4,2,128,128]{4,3,2,0,1:T(8,128)(2,1)}, s32[]{:T(128)}) %tuple.101), condition=%wide.while_cond, body=%wide.while_body.sunk | while | flops 2 | bytes 525937 | solution.py:102
  107.1 5.1 %bitcast_convert_fusion.20 = (f32[16,2,128,128]{3,2,1,0:T(8,128)}, f32[16,2,128,128]{3,2,1,0:T(8,128)}, f32[16,2,128,128]{3,2,1,0:T(8,128)}, f32[16,2,128,128]{3,2,1,0:T(8,128)S(1)}) fusion(bf16[16,4,2,128,128]{4,3,2,0,1:T(8,128)(2,1)} %get-tuple-element.13), kind=kLoop, calls=%fused_computation.200 | loop fusion | flops 2097152 | bytes 12582912 | tf_op jit(solution)/shard_map/convert_element_type | solution.py:92
  117.4 2.6 subtract_convert_fusion.13
  122.1 2.6 subtract_convert_fusion.12
  124.6 3.0 convolution_bitcast_fusion.15
  127.7 2.8 gather_fusion.1
  130.5 3.1 fusion.107
  133.5 4.1 convolution_bitcast_fusion.14
  137.7 5.4 %add_convert_fusion.9 = (bf16[16,1,128,128]{3,2,1,0:T(8,128)(2,1)}, bf16[16,1,128,128]{3,2,1,0:T(8,128)(2,1)}, f32[16,1,128,128]{3,2,1,0:T(8,128)}, f32[16,1,128,128]{3,2,1,0:T(8,128)}) fusion(f32[16,2,128,128]{3,2,1,0:T(8,128)} %convolution_bitcast_fusion.14, f32[16,2,128,128]{3,2,1,0:T(8,128)} %get-tuple-element.99, ...), kind=kLoop, calls=%fused_computation.251 | loop fusion | flops 3670016 | bytes 9437184 | tf_op jit(solution)/shard_map/convert.26
  143.1 3.3 convolution_bitcast_fusion.8
  146.4 5.4 %add_convert_fusion.8 = (bf16[16,1,128,128]{3,2,1,0:T(8,128)(2,1)}, bf16[16,1,128,128]{3,2,1,0:T(8,128)(2,1)}, f32[16,1,128,128]{3,2,1,0:T(8,128)}, f32[16,1,128,128]{3,2,1,0:T(8,128)}) fusion(f32[16,2,128,128]{3,2,1,0:T(8,128)} %convolution_bitcast_fusion.8, f32[16,2,128,128]{3,2,1,0:T(8,128)} %get-tuple-element.100, ...), kind=kLoop, calls=%fused_computation.249 | loop fusion | flops 3670016 | bytes 9437184 | tf_op jit(solution)/shard_map/convert.24
  151.9 3.3 convolution_bitcast_fusion.7
  155.2 4.7 %add_convert_fusion.7 = (bf16[16,1,128,128]{3,2,1,0:T(8,128)(2,1)}, bf16[16,1,128,128]{3,2,1,0:T(8,128)(2,1)}, f32[16,1,128,128]{3,2,1,0:T(8,128)}, f32[16,1,128,128]{3,2,1,0:T(8,128)}) fusion(f32[16,2,128,128]{3,2,1,0:T(8,128)} %convolution_bitcast_fusion.7, f32[16,2,128,128]{3,2,1,0:T(8,128)} %get-tuple-element.101, ...), kind=kLoop, calls=%fused_computation.247 | loop fusion | flops 3670016 | bytes 9437184 | tf_op jit(solution)/shard_map/convert.22
  167.4 6.4 %fusion.359 = (bf16[16,4,2,128,128]{4,3,2,0,1:T(8,128)(2,1)}, bf16[16,4,2,128,128]{4,3,2,0,1:T(8,128)(2,1)}, bf16[16,4,2,128,128]{4,3,2,0,1:T(8,128)(2,1)}) fusion(f32[16]{0:T(128)S(1)} %copy-done.22, f32[16,1,2,128,128]{4,3,2,0,1:T(8,128)S(1)} %maximum_bitcast_fusion.3, f32[16,1,2,128,128]{4,3,2,0,1:T(8,128)S(1)} %maximum_bitcast_fusion.2, ...), kind=kLoop, calls=%fused_computation.482 | loop fusion | flops 23068672 | bytes 20971584 | tf_op jit(solution)/shard_map/convert_element_type | solution.py:125
  173.8 8.1 %fusion.8 = f32[4,2,256,256,1]{3,2,4,1,0:T(8,128)} fusion(bf16[16,4,2,128,128]{4,3,2,0,1:T(8,128)(2,1)} %get-tuple-element.61, s32[16,128]{1,0:T(8,128)S(1)} %get-tuple-element.150, s32[16,128]{1,0:T(8,128)S(1)} %copy-done.19), kind=kOutput, calls=%fused_computation.25 | convolution fusion | flops 3226468352 | bytes 6307840 | tf_op jit(solution)/shard_map/hfi,fscik->schk/dot_general | solution.py:130
  181.9 8.2 %fusion.6 = f32[4,2,256,256,1]{3,2,4,1,0:T(8,128)} fusion(bf16[16,4,2,128,128]{4,3,2,0,1:T(8,128)(2,1)} %get-tuple-element.62, s32[16,128]{1,0:T(8,128)S(1)} %get-tuple-element.150, s32[16,128]{1,0:T(8,128)S(1)} %copy-done.19), kind=kOutput, calls=%fused_computation.22 | convolution fusion | flops 3226468352 | bytes 6307840 | tf_op jit(solution)/shard_map/hfi,fscik->schk/dot_general | solution.py:130
  190.1 8.3 %fusion.39 = f32[4,2,256,256]{2,3,1,0:T(8,128)S(1)} fusion(f32[4,2,256,256,1]{3,2,4,1,0:T(8,128)} %fusion.6, f32[4,2,256,256,1]{3,2,4,1,0:T(8,128)} %fusion.8, bf16[16,4,2,128,128]{4,3,2,0,1:T(8,128)(2,1)} %get-tuple-element.60, s32[16,128]{1,0:T(8,128)S(1)} %get-tuple-element.150, s32[16,128]{1,0:T(8,128)} %get-tuple-element.151), kind=kOutput, calls=%fused_computation.70 | convolution fusion | flops 3227516928 | bytes 10502144 | tf_op jit(solution)/shard_map/hfi,fscik->schk/dot_general | solution.py:130
  205.3 36.0 %reduce-scatter.3.cloned.1.call-done = f32[1,2,256,128]{2,3,1,0:T(8,128)} async-done(((f32[4,2,256,128]{2,3,1,0:T(8,128)}), f32[1,2,256,128]{2,3,1,0:T(8,128)}) %reduce-scatter.3.cloned.1.call-update) | async-done | bytes 262160 | tf_op jit(solution)/shard_map/reduce_scatter | solution.py:137
  242.4 12.8 %all_gather.7 = bf16[4,2,256,128]{3,2,1,0:T(8,128)(2,1)S(1)} all-gather(bf16[1,2,256,128]{3,2,1,0:T(8,128)(2,1)S(1)} %copy.237), channel_id=1, replica_groups=mesh['tile'=32,'cuts'=4] {'cuts'}, dimensions={0}, use_global_device_ids=true | all-gather | bytes 655360 | tf_op jit(solution)/shard_map/all_gather | solution.py:201
  256.5 2.5 collective-permute-done.2
  259.1 3.0 broadcast.645.clone
  262.1 46.3 %while.3 = (s32[]{:T(128)}, bf16[4,2,256,256]{3,2,1,0:T(8,128)(2,1)S(1)}, s32[16,4]{0,1:T(4,128)S(1)}, bf16[16,4,2,128,128]{4,3,2,0,1:T(8,128)(2,1)}, s32[]{:T(128)}) while((s32[]{:T(128)}, bf16[4,2,256,256]{3,2,1,0:T(8,128)(2,1)S(1)}, s32[16,4]{0,1:T(4,128)S(1)}, bf16[16,4,2,128,128]{4,3,2,0,1:T(8,128)(2,1)}, s32[]{:T(128)}) %tuple.111), condition=%wide.while_cond.1, body=%wide.while_body.1.sunk | while | flops 2 | bytes 525937 | solution.py:102
  262.8 2.2 bitcast_dynamic-update-slice_fusion.5
  265.7 2.2 bitcast_dynamic-update-slice_fusion.5
  268.6 2.2 bitcast_dynamic-update-slice_fusion.5
  271.5 2.2 bitcast_dynamic-update-slice_fusion.5
  274.4 2.2 bitcast_dynamic-update-slice_fusion.5
  277.3 2.2 bitcast_dynamic-update-slice_fusion.5
  280.2 2.3 bitcast_dynamic-update-slice_fusion.5
  286.0 2.2 bitcast_dynamic-update-slice_fusion.5
  288.8 2.2 bitcast_dynamic-update-slice_fusion.5
  291.7 2.2 bitcast_dynamic-update-slice_fusion.5
  294.6 2.2 bitcast_dynamic-update-slice_fusion.5
  297.5 2.2 bitcast_dynamic-update-slice_fusion.5
  300.4 2.2 bitcast_dynamic-update-slice_fusion.5
  303.3 2.2 bitcast_dynamic-update-slice_fusion.5
  306.2 2.2 bitcast_dynamic-update-slice_fusion.5
  308.4 5.2 %bitcast_convert_fusion.16 = (f32[16,2,128,128]{3,2,1,0:T(8,128)}, f32[16,2,128,128]{3,2,1,0:T(8,128)}, f32[16,2,128,128]{3,2,1,0:T(8,128)}, f32[16,2,128,128]{3,2,1,0:T(8,128)S(1)}) fusion(bf16[16,4,2,128,128]{4,3,2,0,1:T(8,128)(2,1)} %get-tuple-element.21), kind=kLoop, calls=%fused_computation.194 | loop fusion | flops 2097152 | bytes 12582912 | tf_op jit(solution)/shard_map/convert_element_type | solution.py:92
  316.8 2.9 subtract_convert_fusion.7
  319.7 3.3 convolution_bitcast_fusion.4
  323.0 3.5 subtract_convert_fusion.6
  326.6 3.3 convolution_bitcast_fusion.3
  329.9 3.6 subtract_convert_fusion.5
  333.4 3.3 convolution_bitcast_fusion.13
  336.8 3.1 fusion.101
  339.9 3.9 convolution_bitcast_fusion.12
  343.8 5.0 %add_convert_fusion.2 = (bf16[16,1,128,128]{3,2,1,0:T(8,128)(2,1)}, bf16[16,1,128,128]{3,2,1,0:T(8,128)(2,1)}, f32[16,1,128,128]{3,2,1,0:T(8,128)S(1)}, f32[16,1,128,128]{3,2,1,0:T(8,128)}) fusion(f32[16,2,128,128]{3,2,1,0:T(8,128)} %convolution_bitcast_fusion.12, f32[16,2,128,128]{3,2,1,0:T(8,128)} %get-tuple-element.77, ...), kind=kLoop, calls=%fused_computation.217 | loop fusion | flops 3670016 | bytes 9437184 | tf_op jit(solution)/shard_map/convert.12
  348.8 3.3 convolution_bitcast_fusion.2
  352.1 5.4 %add_convert_fusion.1 = (bf16[16,1,128,128]{3,2,1,0:T(8,128)(2,1)}, bf16[16,1,128,128]{3,2,1,0:T(8,128)(2,1)}, f32[16,1,128,128]{3,2,1,0:T(8,128)}, f32[16,1,128,128]{3,2,1,0:T(8,128)}) fusion(f32[16,2,128,128]{3,2,1,0:T(8,128)} %convolution_bitcast_fusion.2, f32[16,2,128,128]{3,2,1,0:T(8,128)} %get-tuple-element.78, ...), kind=kLoop, calls=%fused_computation.215 | loop fusion | flops 3670016 | bytes 9437184 | tf_op jit(solution)/shard_map/convert.10
  357.5 3.3 convolution_bitcast_fusion.1
  360.8 4.6 %add_convert_fusion = (bf16[16,1,128,128]{3,2,1,0:T(8,128)(2,1)}, bf16[16,1,128,128]{3,2,1,0:T(8,128)(2,1)}, f32[16,1,128,128]{3,2,1,0:T(8,128)}, f32[16,1,128,128]{3,2,1,0:T(8,128)}) fusion(f32[16,2,128,128]{3,2,1,0:T(8,128)} %convolution_bitcast_fusion.1, f32[16,2,128,128]{3,2,1,0:T(8,128)} %get-tuple-element.79, ...), kind=kLoop, calls=%fused_computation.213 | loop fusion | flops 3670016 | bytes 9437184 | tf_op jit(solution)/shard_map/convert.8
  372.2 6.4 %fusion.358 = (bf16[16,4,2,128,128]{4,3,2,0,1:T(8,128)(2,1)}, bf16[16,4,2,128,128]{4,3,2,0,1:T(8,128)(2,1)}, bf16[16,4,2,128,128]{4,3,2,0,1:T(8,128)(2,1)}) fusion(f32[16]{0:T(128)S(1)} %copy-done.22, f32[16,1,2,128,128]{4,3,2,0,1:T(8,128)S(1)} %maximum_bitcast_fusion.7, f32[16,1,2,128,128]{4,3,2,0,1:T(8,128)S(1)} %maximum_bitcast_fusion.6, ...), kind=kLoop, calls=%fused_computation.481 | loop fusion | flops 23068672 | bytes 20971584 | tf_op jit(solution)/shard_map/convert_element_type | solution.py:125
  378.6 8.1 %fusion.2 = f32[4,2,256,256,1]{3,2,4,1,0:T(8,128)} fusion(bf16[16,4,2,128,128]{4,3,2,0,1:T(8,128)(2,1)} %get-tuple-element.58, s32[16,128]{1,0:T(8,128)S(1)} %get-tuple-element.150, s32[16,128]{1,0:T(8,128)S(1)} %copy-done.20), kind=kOutput, calls=%fused_computation.17 | convolution fusion | flops 3226468352 | bytes 6307840 | tf_op jit(solution)/shard_map/hfi,fscik->schk/dot_general | solution.py:130
  386.8 8.2 %fusion = f32[4,2,256,256,1]{3,2,4,1,0:T(8,128)} fusion(bf16[16,4,2,128,128]{4,3,2,0,1:T(8,128)(2,1)} %get-tuple-element.59, s32[16,128]{1,0:T(8,128)S(1)} %get-tuple-element.150, s32[16,128]{1,0:T(8,128)S(1)} %copy-done.20), kind=kOutput, calls=%fused_computation.14 | convolution fusion | flops 3226468352 | bytes 6307840 | tf_op jit(solution)/shard_map/hfi,fscik->schk/dot_general | solution.py:130
  395.0 8.4 %fusion.38 = f32[4,2,256,256]{2,3,1,0:T(8,128)S(1)} fusion(f32[4,2,256,256,1]{3,2,4,1,0:T(8,128)} %fusion, f32[4,2,256,256,1]{3,2,4,1,0:T(8,128)} %fusion.2, bf16[16,4,2,128,128]{4,3,2,0,1:T(8,128)(2,1)} %get-tuple-element.57, s32[16,128]{1,0:T(8,128)S(1)} %get-tuple-element.150, s32[16,128]{1,0:T(8,128)S(1)} %copy-done.20), kind=kOutput, calls=%fused_computation.65 | convolution fusion | flops 3227516928 | bytes 10502144 | tf_op jit(solution)/shard_map/hfi,fscik->schk/dot_general | solution.py:130
  403.5 8.7 %collective-permute-start.3 = (f32[4,2,256,128]{2,3,1,0:T(8,128)S(1)}, f32[4,2,256,128]{2,3,1,0:T(8,128)S(1)}, u32[]{:S(2)}, u32[]{:S(2)}) collective-permute-start(f32[4,2,256,128]{2,3,1,0:T(8,128)S(1)} %slice.507), channel_id=1, source_target_pairs={{0,4},{4,8},{8,12},{12,16},{16,20},{20,24},{24,28},{28,32},{32,36}... | collective-permute-start | bytes 3145736 | tf_op jit(solution)/shard_map/ppermute | solution.py:15
  415.6 33.9 %reduce-scatter.5.cloned.1.call-done = f32[1,2,256,128]{2,3,1,0:T(8,128)} async-done(((f32[4,2,256,128]{2,3,1,0:T(8,128)}), f32[1,2,256,128]{2,3,1,0:T(8,128)}) %reduce-scatter.5.cloned.1.call-update) | async-done | bytes 262160 | tf_op jit(solution)/shard_map/reduce_scatter | solution.py:137
  (219 shorter events, 110.2 us)
Async XLA Ops:
  20.9 38.2 %collective-permute-start = (bf16[4,2,256,128]{3,2,1,0:T(8,128)(2,1)S(1)}, bf16[4,2,256,128]{3,2,1,0:T(8,128)(2,1)S(1)}, u32[]{:S(2)}, u32[]{:S(2)}) collective-permute-start(bf16[4,2,256,128]{3,2,1,0:T(8,128)(2,1)S(1)} %all_gather.6), channel_id=1, source_target_pairs={{4,0},{8,4},{12,8},{16,12},{20,16},{24,20},{28,24},{32,28},{36,32}... | collective-permute-start | bytes 1572872 | tf_op jit(solution)/shard_map/ppermute | solution.py:15
  34.1 93.5 %all-to-all-start = ((f32[32,2,128,128]{3,2,1,0:T(8,128)}), f32[32,2,128,128]{3,2,1,0:T(8,128)}, u32[]{:S(2)}, u32[]{:S(2)}) async-start(f32[32,2,128,128]{3,2,1,0:T(8,128)} %broadcast_select_fusion), calls=%async_computation | async-start | bytes 8388608 | tf_op jit(solution)/shard_map/all_to_all | solution.py:180
  43.1 198.1 %reduce-scatter.3.cloned.1.call-start = ((), (), s32[]{:S(2)}) async-start(), calls=%async_computation.3 | async-start | bytes 1310720 | tf_op jit(solution)/shard_map/reduce_scatter | solution.py:137
  43.8 15.3 %copy-start.18 = (f32[2,128,128]{2,1,0:T(8,128)S(1)}, f32[2,128,128]{2,1,0:T(8,128)}, u32[]{:S(2)}) copy-start(f32[2,128,128]{2,1,0:T(8,128)} %param.8) | copy-start | bytes 393220
  162.1 1.2 copy-start.9
  162.1 1.5 copy-start.10
  163.6 1.2 copy-start.5
  163.6 1.5 copy-start.6
  165.2 1.2 copy-start.1
  165.2 1.5 copy-start.2
  166.7 0.7 copy-start.22
  167.4 6.4 %copy-start.19 = (s32[16,128]{1,0:T(8,128)S(1)}, s32[16,128]{1,0:T(8,128)}, u32[]{:S(2)}) copy-start(s32[16,128]{1,0:T(8,128)} %get-tuple-element.151) | copy-start | bytes 24580
  198.6 4.4 collective-permute-start.1
  204.1 245.3 %reduce-scatter.5.cloned.1.call-start = ((), (), s32[]{:S(2)}) async-start(), calls=%async_computation.4 | async-start | bytes 1310720 | tf_op jit(solution)/shard_map/reduce_scatter | solution.py:137
  205.3 51.2 %copy-start.11 = (f32[1,2,256,128]{2,3,1,0:T(8,128)}, f32[1,2,256,128]{2,3,1,0:T(8,128)S(1)}, u32[]{:S(2)}) copy-start(f32[1,2,256,128]{2,3,1,0:T(8,128)S(1)} %copy.236) | copy-start | bytes 786436
  255.2 3.8 collective-permute-start.2
  329.9 3.6 copy-start.15
  329.9 3.6 copy-start.16
  333.4 3.3 copy-start.21
  336.8 3.1 copy-start.13
  336.8 3.1 copy-start.14
  367.7 1.2 copy-start.7
  367.7 1.5 copy-start.8
  369.2 1.2 copy-start.3
  369.2 1.5 copy-start.4
  370.8 1.2 copy-start
  372.2 6.4 %copy-start.20 = (s32[16,128]{1,0:T(8,128)S(1)}, s32[16,128]{1,0:T(8,128)}, u32[]{:S(2)}) copy-start(s32[16,128]{1,0:T(8,128)} %get-tuple-element.151) | copy-start | bytes 24580
  403.5 46.0 %copy-start.12 = (f32[1,2,256,128]{2,3,1,0:T(8,128)S(1)}, f32[1,2,256,128]{2,3,1,0:T(8,128)}, u32[]{:S(2)}) copy-start(f32[1,2,256,128]{2,3,1,0:T(8,128)} %copy-done.11) | copy-start | bytes 786436
  403.5 46.0 %copy-start.17 = (f32[1,2,256,128]{2,3,1,0:T(8,128)S(1)}, f32[1,2,256,128]{2,3,1,0:T(8,128)}, u32[]{:S(2)}) copy-start(f32[1,2,256,128]{2,3,1,0:T(8,128)} %reduce-scatter.3.cloned.1.call-done) | copy-start | bytes 786436
  403.5 10.9 %collective-permute-start.3 = (f32[4,2,256,128]{2,3,1,0:T(8,128)S(1)}, f32[4,2,256,128]{2,3,1,0:T(8,128)S(1)}, u32[]{:S(2)}, u32[]{:S(2)}) collective-permute-start(f32[4,2,256,128]{2,3,1,0:T(8,128)S(1)} %slice.507), channel_id=1, source_target_pairs={{0,4},{4,8},{8,12},{12,16},{16,20},{20,24},{24,28},{28,32},{32,36}... | collective-permute-start | bytes 3145736 | tf_op jit(solution)/shard_map/ppermute | solution.py:15
Sparse Core Ops, SparseCore 0:
  204.3 36.9 reduce-scatter.2
  415.7 33.6 reduce-scatter.4
where the time goes:
time: 466 us; the launch traced here: 459 us
  local copies, waits for them, and re-layouts  127 us (27%)
  matrix products  96.5 us (21%)
  other arithmetic  95.2 us (20%)
  waiting for transfers between devices  76.8 us (16%)
  blocking collectives  26.2 us (6%)
  starting transfers between devices  22.6 us (5%)
  between operations  14.4 us (3%)
    gather x96, local copies, waits for them, and re-layouts  90.8 us
    reduce_scatter x2, waiting for transfers between devices, reduce_gradient(): return lax.psum_scatter(term_part, 'cuts', scatter_dimension=0, tiled=True)  69.8 us
    another operation x18, other arithmetic  50.1 us
    dot_general x6, matrix products, place_patches(): jnp.einsum('hfi,fscik->schk', row_onehot, placed_cols, preferred_element_...  49.4 us
    dot_general x16, matrix products, right_product(): jnp.einsum('fcij,cjdk->fdik', field.astype(jnp.bfloat16), table, preferre...  45.2 us
    all_gather x2, blocking collectives, body(): lax.all_gather(current.astype(jnp.bfloat16), 'cuts', axis=0, tiled=True)  26.2 us
    unnamed x49, local copies, waits for them, and re-layouts  15.1 us
    ppermute x4, starting transfers between devices, passed_along(): return lax.ppermute(x, axis, pairs)  13.5 us
  transfers between devices with their start and end apart: 7, of which 5 were waited for; matrix products, arithmetic and copies ran while one was open for 21% of the time, Pallas kernels for 0%

commit v1 on v0

--- a/solution.py
+++ b/solution.py
@@ -198,7 +198,12 @@
     tables = make_tables(frame_side)
     current = object_slices
     for turn in range(ITERS):
-        stacked = lax.all_gather(current.astype(jnp.bfloat16), "cuts", axis=0, tiled=True)
+        stacked = jnp.concatenate(
+            lax.all_to_all(
+                jnp.stack([current.astype(jnp.bfloat16)] * lax.axis_size("cuts")), "cuts", 0, 0
+            ),
+            axis=0,
+        )
         next_rim = passed_along(stacked, "tile", -1)
         panel = jnp.concatenate([stacked, next_rim], axis=-1)
         windows = cut_windows(panel, frame_rows, frame_cols, frame_side)

time: 466 us -> 505 us (1.084)
  starting transfers between devices: 22.6 us -> 78.2 us
  blocking collectives: 26.2 us -> 10.7 us
    ppermute x4, starting transfers between devices: 13.5 us -> 65.1 us  [passed_along(): return lax.ppermute(x, axis, pairs)]
    all_gather x2 -> x0, blocking collectives: 26.2 us -> none  [body(): lax.all_gather(current.astype(jnp.bfloat16), 'cuts', axis=0, tiled=True)]
    all_to_all x0 -> x1, blocking collectives: none -> 10.7 us  [body(): lax.all_to_all(jnp.stack([current.astype(jnp.bfloat16)] * lax.axis_size('...]
    unnamed x49 -> x53, local copies, waits for them, and re-layouts: 15.1 us -> 15.1 us
  transfers between devices with their start and end apart: 7 -> 8, of which waited for: 5 -> 6; matrix products, arithmetic and copies ran while one was open for 21% -> 19% of each run, Pallas kernels for 0% -> 0%
where the time goes in v1:
time: 505 us; the launch traced here: 497 us
  local copies, waits for them, and re-layouts  126 us (25%)
  matrix products  96.4 us (19%)
  other arithmetic  94.5 us (19%)
  starting transfers between devices  78.2 us (15%)
  waiting for transfers between devices  76.3 us (15%)
  between operations  14.4 us (3%)
  blocking collectives  10.7 us (2%)
    gather x96, local copies, waits for them, and re-layouts  91 us
    reduce_scatter x2, waiting for transfers between devices, reduce_gradient(): return lax.psum_scatter(term_part, 'cuts', scatter_dimension=0, tiled=True)  67.6 us
    ppermute x4, starting transfers between devices, passed_along(): return lax.ppermute(x, axis, pairs)  65.1 us
    another operation x18, other arithmetic  50.2 us
    dot_general x6, matrix products, place_patches(): jnp.einsum('hfi,fscik->schk', row_onehot, placed_cols, preferred_element_...  49.3 us
    dot_general x16, matrix products, right_product(): jnp.einsum('fcij,cjdk->fdik', field.astype(jnp.bfloat16), table, preferre...  45.2 us
    unnamed x53, local copies, waits for them, and re-layouts  15.1 us
    convert_element_type x2, other arithmetic, place_patches(): piece_part = remain.astype(jnp.bfloat16)  12.7 us
  transfers between devices with their start and end apart: 8, of which 6 were waited for; matrix products, arithmetic and copies ran while one was open for 19% of the time, Pallas kernels for 0%

profile of v1, /device:TPU:0, one launch (start us, length us, event | category | flops | bytes accessed | tf_op | source)
XLA Modules:
  0.0 497.1 jit_solution(233483592203872304)
XLA Ops:
  8.4 4.6 all-to-all-start
  16.6 4.3 scatter_custom_fusion
  24.7 4.8 scatter_custom_fusion.2
  29.5 2.8 gather_fusion
  33.1 4.5 broadcast_select_fusion
  37.6 8.4 %all-to-all-start.1 = ((f32[32,2,128,128]{3,2,1,0:T(8,128)}), f32[32,2,128,128]{3,2,1,0:T(8,128)}, u32[]{:S(2)}, u32[]{:S(2)}) async-start(f32[32,2,128,128]{3,2,1,0:T(8,128)} %broadcast_select_fusion), calls=%async_computation.1 | async-start | bytes 8388608 | tf_op jit(solution)/shard_map/all_to_all | solution.py:180
  50.1 3.1 broadcast.651.clone2
  53.1 44.5 %while.2 = (s32[]{:T(128)}, bf16[4,2,256,256]{3,2,1,0:T(8,128)(2,1)S(1)}, s32[16,4]{0,1:T(4,128)S(1)}, bf16[16,4,2,128,128]{4,3,2,0,1:T(8,128)(2,1)}, s32[]{:T(128)}) while((s32[]{:T(128)}, bf16[4,2,256,256]{3,2,1,0:T(8,128)(2,1)S(1)}, s32[16,4]{0,1:T(4,128)S(1)}, bf16[16,4,2,128,128]{4,3,2,0,1:T(8,128)(2,1)}, s32[]{:T(128)}) %tuple.99), condition=%wide.while_cond, body=%wide.while_body.sunk | while | flops 2 | bytes 525937 | solution.py:102
  97.7 5.1 %bitcast_convert_fusion.20 = (f32[16,2,128,128]{3,2,1,0:T(8,128)}, f32[16,2,128,128]{3,2,1,0:T(8,128)}, f32[16,2,128,128]{3,2,1,0:T(8,128)}, f32[16,2,128,128]{3,2,1,0:T(8,128)S(1)}) fusion(bf16[16,4,2,128,128]{4,3,2,0,1:T(8,128)(2,1)} %get-tuple-element.13), kind=kLoop, calls=%fused_computation.200 | loop fusion | flops 2097152 | bytes 12582912 | tf_op jit(solution)/shard_map/convert_element_type | solution.py:92
  107.9 2.6 subtract_convert_fusion.13
  112.6 2.6 subtract_convert_fusion.12
  115.2 3.0 convolution_bitcast_fusion.15
  118.2 2.8 gather_fusion.1
  121.0 3.1 fusion.107
  124.1 4.1 convolution_bitcast_fusion.14
  128.2 5.5 %add_convert_fusion.9 = (bf16[16,1,128,128]{3,2,1,0:T(8,128)(2,1)}, bf16[16,1,128,128]{3,2,1,0:T(8,128)(2,1)}, f32[16,1,128,128]{3,2,1,0:T(8,128)}, f32[16,1,128,128]{3,2,1,0:T(8,128)}) fusion(f32[16,2,128,128]{3,2,1,0:T(8,128)} %convolution_bitcast_fusion.14, f32[16,2,128,128]{3,2,1,0:T(8,128)} %get-tuple-element.91, ...), kind=kLoop, calls=%fused_computation.251 | loop fusion | flops 3670016 | bytes 9437184 | tf_op jit(solution)/shard_map/convert.26
  133.7 3.3 convolution_bitcast_fusion.8
  137.0 5.4 %add_convert_fusion.8 = (bf16[16,1,128,128]{3,2,1,0:T(8,128)(2,1)}, bf16[16,1,128,128]{3,2,1,0:T(8,128)(2,1)}, f32[16,1,128,128]{3,2,1,0:T(8,128)}, f32[16,1,128,128]{3,2,1,0:T(8,128)}) fusion(f32[16,2,128,128]{3,2,1,0:T(8,128)} %convolution_bitcast_fusion.8, f32[16,2,128,128]{3,2,1,0:T(8,128)} %get-tuple-element.92, ...), kind=kLoop, calls=%fused_computation.249 | loop fusion | flops 3670016 | bytes 9437184 | tf_op jit(solution)/shard_map/convert.24
  142.5 3.3 convolution_bitcast_fusion.7
  145.8 4.7 add_convert_fusion.7
  158.0 6.4 %fusion.358 = (bf16[16,4,2,128,128]{4,3,2,0,1:T(8,128)(2,1)}, bf16[16,4,2,128,128]{4,3,2,0,1:T(8,128)(2,1)}, bf16[16,4,2,128,128]{4,3,2,0,1:T(8,128)(2,1)}) fusion(f32[16]{0:T(128)S(1)} %copy-done.24, f32[16,1,2,128,128]{4,3,2,0,1:T(8,128)S(1)} %maximum_bitcast_fusion.3, f32[16,1,2,128,128]{4,3,2,0,1:T(8,128)S(1)} %maximum_bitcast_fusion.2, ...), kind=kLoop, calls=%fused_computation.483 | loop fusion | flops 23068672 | bytes 20971584 | tf_op jit(solution)/shard_map/convert_element_type | solution.py:125
  164.4 8.1 %fusion.8 = f32[4,2,256,256,1]{3,2,4,1,0:T(8,128)} fusion(bf16[16,4,2,128,128]{4,3,2,0,1:T(8,128)(2,1)} %get-tuple-element.53, s32[16,128]{1,0:T(8,128)S(1)} %get-tuple-element.142, s32[16,128]{1,0:T(8,128)S(1)} %copy-done.21), kind=kOutput, calls=%fused_computation.25 | convolution fusion | flops 3226468352 | bytes 6307840 | tf_op jit(solution)/shard_map/hfi,fscik->schk/dot_general | solution.py:130
  172.5 8.2 %fusion.6 = f32[4,2,256,256,1]{3,2,4,1,0:T(8,128)} fusion(bf16[16,4,2,128,128]{4,3,2,0,1:T(8,128)(2,1)} %get-tuple-element.54, s32[16,128]{1,0:T(8,128)S(1)} %get-tuple-element.142, s32[16,128]{1,0:T(8,128)S(1)} %copy-done.21), kind=kOutput, calls=%fused_computation.22 | convolution fusion | flops 3226468352 | bytes 6307840 | tf_op jit(solution)/shard_map/hfi,fscik->schk/dot_general | solution.py:130
  180.7 8.3 %fusion.39 = f32[4,2,256,256]{2,3,1,0:T(8,128)S(1)} fusion(f32[4,2,256,256,1]{3,2,4,1,0:T(8,128)} %fusion.6, f32[4,2,256,256,1]{3,2,4,1,0:T(8,128)} %fusion.8, bf16[16,4,2,128,128]{4,3,2,0,1:T(8,128)(2,1)} %get-tuple-element.52, s32[16,128]{1,0:T(8,128)S(1)} %get-tuple-element.142, s32[16,128]{1,0:T(8,128)} %get-tuple-element.143), kind=kOutput, calls=%fused_computation.70 | convolution fusion | flops 3227516928 | bytes 10502144 | tf_op jit(solution)/shard_map/hfi,fscik->schk/dot_general | solution.py:130
  189.1 53.9 %collective-permute-start.1 = (f32[4,2,256,128]{2,3,1,0:T(8,128)S(1)}, f32[4,2,256,128]{2,3,1,0:T(8,128)S(1)}, u32[]{:S(2)}, u32[]{:S(2)}) collective-permute-start(f32[4,2,256,128]{2,3,1,0:T(8,128)S(1)} %slice.481), channel_id=1, source_target_pairs={{0,4},{4,8},{8,12},{12,16},{16,20},{20,24},{24,28},{28,32},{32,36}... | collective-permute-start | bytes 3145736 | tf_op jit(solution)/shard_map/ppermute | solution.py:15
  247.6 34.0 %reduce-scatter.3.cloned.1.call-done = f32[1,2,256,128]{2,3,1,0:T(8,128)} async-done(((f32[4,2,256,128]{2,3,1,0:T(8,128)}), f32[1,2,256,128]{2,3,1,0:T(8,128)}) %reduce-scatter.3.cloned.1.call-update) | async-done | bytes 262160 | tf_op jit(solution)/shard_map/reduce_scatter | solution.py:137
  282.8 10.7 %all_to_all.15 = bf16[4,1,2,256,128]{4,3,2,1,0:T(8,128)(2,1)S(1)} all-to-all(bf16[4,1,2,256,128]{4,3,2,1,0:T(8,128)(2,1)S(1)} %stack.310), channel_id=1, replica_groups=mesh['tile'=32,'cuts'=4] {'cuts'}, dimensions={0} | all-to-all | bytes 1048576 | tf_op jit(solution)/shard_map/all_to_all | solution.py:202
  294.8 2.5 collective-permute-done.2
  297.4 3.0 broadcast.651.clone
  300.4 46.7 %while.3 = (s32[]{:T(128)}, bf16[4,2,256,256]{3,2,1,0:T(8,128)(2,1)S(1)}, s32[16,4]{0,1:T(4,128)S(1)}, bf16[16,4,2,128,128]{4,3,2,0,1:T(8,128)(2,1)}, s32[]{:T(128)}) while((s32[]{:T(128)}, bf16[4,2,256,256]{3,2,1,0:T(8,128)(2,1)S(1)}, s32[16,4]{0,1:T(4,128)S(1)}, bf16[16,4,2,128,128]{4,3,2,0,1:T(8,128)(2,1)}, s32[]{:T(128)}) %tuple.109), condition=%wide.while_cond.1, body=%wide.while_body.1.sunk | while | flops 2 | bytes 525937 | solution.py:102
  301.1 2.3 bitcast_dynamic-update-slice_fusion.5
  304.1 2.3 bitcast_dynamic-update-slice_fusion.5
  307.0 2.2 bitcast_dynamic-update-slice_fusion.5
  309.9 2.2 bitcast_dynamic-update-slice_fusion.5
  312.8 2.3 bitcast_dynamic-update-slice_fusion.5
  315.8 2.3 bitcast_dynamic-update-slice_fusion.5
  324.5 2.2 bitcast_dynamic-update-slice_fusion.5
  327.4 2.2 bitcast_dynamic-update-slice_fusion.5
  330.3 2.2 bitcast_dynamic-update-slice_fusion.5
  333.2 2.3 bitcast_dynamic-update-slice_fusion.5
  336.2 2.2 bitcast_dynamic-update-slice_fusion.5
  339.1 2.2 bitcast_dynamic-update-slice_fusion.5
  342.0 2.2 bitcast_dynamic-update-slice_fusion.5
  344.9 2.2 bitcast_dynamic-update-slice_fusion.5
  347.1 5.2 %bitcast_convert_fusion.16 = (f32[16,2,128,128]{3,2,1,0:T(8,128)}, f32[16,2,128,128]{3,2,1,0:T(8,128)}, f32[16,2,128,128]{3,2,1,0:T(8,128)}, f32[16,2,128,128]{3,2,1,0:T(8,128)S(1)}) fusion(bf16[16,4,2,128,128]{4,3,2,0,1:T(8,128)(2,1)} %get-tuple-element.21), kind=kLoop, calls=%fused_computation.194 | loop fusion | flops 2097152 | bytes 12582912 | tf_op jit(solution)/shard_map/convert_element_type | solution.py:92
  355.6 2.9 subtract_convert_fusion.7
  358.5 3.3 convolution_bitcast_fusion.4
  361.8 3.5 subtract_convert_fusion.6
  365.4 3.3 convolution_bitcast_fusion.3
  368.7 3.6 subtract_convert_fusion.5
  372.3 3.3 convolution_bitcast_fusion.13
  375.6 3.1 fusion.101
  378.7 3.9 convolution_bitcast_fusion.12
  382.6 5.0 %add_convert_fusion.2 = (bf16[16,1,128,128]{3,2,1,0:T(8,128)(2,1)}, bf16[16,1,128,128]{3,2,1,0:T(8,128)(2,1)}, f32[16,1,128,128]{3,2,1,0:T(8,128)S(1)}, f32[16,1,128,128]{3,2,1,0:T(8,128)}) fusion(f32[16,2,128,128]{3,2,1,0:T(8,128)} %convolution_bitcast_fusion.12, f32[16,2,128,128]{3,2,1,0:T(8,128)} %get-tuple-element.69, ...), kind=kLoop, calls=%fused_computation.217 | loop fusion | flops 3670016 | bytes 9437184 | tf_op jit(solution)/shard_map/convert.12
  387.6 3.3 convolution_bitcast_fusion.2
  390.9 5.4 %add_convert_fusion.1 = (bf16[16,1,128,128]{3,2,1,0:T(8,128)(2,1)}, bf16[16,1,128,128]{3,2,1,0:T(8,128)(2,1)}, f32[16,1,128,128]{3,2,1,0:T(8,128)}, f32[16,1,128,128]{3,2,1,0:T(8,128)}) fusion(f32[16,2,128,128]{3,2,1,0:T(8,128)} %convolution_bitcast_fusion.2, f32[16,2,128,128]{3,2,1,0:T(8,128)} %get-tuple-element.70, ...), kind=kLoop, calls=%fused_computation.215 | loop fusion | flops 3670016 | bytes 9437184 | tf_op jit(solution)/shard_map/convert.10
  396.4 3.3 convolution_bitcast_fusion.1
  399.7 4.6 add_convert_fusion
  411.1 6.4 %fusion.357 = (bf16[16,4,2,128,128]{4,3,2,0,1:T(8,128)(2,1)}, bf16[16,4,2,128,128]{4,3,2,0,1:T(8,128)(2,1)}, bf16[16,4,2,128,128]{4,3,2,0,1:T(8,128)(2,1)}) fusion(f32[16]{0:T(128)S(1)} %copy-done.24, f32[16,1,2,128,128]{4,3,2,0,1:T(8,128)S(1)} %maximum_bitcast_fusion.7, f32[16,1,2,128,128]{4,3,2,0,1:T(8,128)S(1)} %maximum_bitcast_fusion.6, ...), kind=kLoop, calls=%fused_computation.482 | loop fusion | flops 23068672 | bytes 20971584 | tf_op jit(solution)/shard_map/convert_element_type | solution.py:125
  417.5 8.1 %fusion.2 = f32[4,2,256,256,1]{3,2,4,1,0:T(8,128)} fusion(bf16[16,4,2,128,128]{4,3,2,0,1:T(8,128)(2,1)} %get-tuple-element.50, s32[16,128]{1,0:T(8,128)S(1)} %get-tuple-element.142, s32[16,128]{1,0:T(8,128)S(1)} %copy-done.22), kind=kOutput, calls=%fused_computation.17 | convolution fusion | flops 3226468352 | bytes 6307840 | tf_op jit(solution)/shard_map/hfi,fscik->schk/dot_general | solution.py:130
  425.6 8.2 %fusion = f32[4,2,256,256,1]{3,2,4,1,0:T(8,128)} fusion(bf16[16,4,2,128,128]{4,3,2,0,1:T(8,128)(2,1)} %get-tuple-element.51, s32[16,128]{1,0:T(8,128)S(1)} %get-tuple-element.142, s32[16,128]{1,0:T(8,128)S(1)} %copy-done.22), kind=kOutput, calls=%fused_computation.14 | convolution fusion | flops 3226468352 | bytes 6307840 | tf_op jit(solution)/shard_map/hfi,fscik->schk/dot_general | solution.py:130
  433.8 8.4 %fusion.38 = f32[4,2,256,256]{2,3,1,0:T(8,128)S(1)} fusion(f32[4,2,256,256,1]{3,2,4,1,0:T(8,128)} %fusion, f32[4,2,256,256,1]{3,2,4,1,0:T(8,128)} %fusion.2, bf16[16,4,2,128,128]{4,3,2,0,1:T(8,128)(2,1)} %get-tuple-element.49, s32[16,128]{1,0:T(8,128)S(1)} %get-tuple-element.142, s32[16,128]{1,0:T(8,128)S(1)} %copy-done.22), kind=kOutput, calls=%fused_computation.65 | convolution fusion | flops 3227516928 | bytes 10502144 | tf_op jit(solution)/shard_map/hfi,fscik->schk/dot_general | solution.py:130
  442.3 8.7 %collective-permute-start.3 = (f32[4,2,256,128]{2,3,1,0:T(8,128)S(1)}, f32[4,2,256,128]{2,3,1,0:T(8,128)S(1)}, u32[]{:S(2)}, u32[]{:S(2)}) collective-permute-start(f32[4,2,256,128]{2,3,1,0:T(8,128)S(1)} %slice.507), channel_id=1, source_target_pairs={{0,4},{4,8},{8,12},{12,16},{16,20},{20,24},{24,28},{28,32},{32,36}... | collective-permute-start | bytes 3145736 | tf_op jit(solution)/shard_map/ppermute | solution.py:15
  454.4 33.6 %reduce-scatter.5.cloned.1.call-done = f32[1,2,256,128]{2,3,1,0:T(8,128)} async-done(((f32[4,2,256,128]{2,3,1,0:T(8,128)}), f32[1,2,256,128]{2,3,1,0:T(8,128)}) %reduce-scatter.5.cloned.1.call-update) | async-done | bytes 262160 | tf_op jit(solution)/shard_map/reduce_scatter | solution.py:137
  (226 shorter events, 110.5 us)
Async XLA Ops:
  6.5 8.1 %copy-start.20 = (s32[1024,2]{0,1:T(2,128)S(1)}, s32[1024,2]{0,1:T(2,128)}, u32[]{:S(2)}) copy-start(s32[1024,2]{0,1:T(2,128)} %param.7) | copy-start | bytes 24580
  8.4 29.2 %all-to-all-start = ((bf16[4,1,2,256,128]{4,3,2,1,0:T(8,128)(2,1)}), bf16[4,1,2,256,128]{4,3,2,1,0:T(8,128)(2,1)S(1)}, u32[]{:S(2)}, u32[]{:S(2)}) async-start(bf16[4,1,2,256,128]{4,3,2,1,0:T(8,128)(2,1)} %stack.278), calls=%async_computation | async-start | bytes 1048576 | tf_op jit(solution)/shard_map/all_to_all | solution.py:202
  13.5 11.1 %copy-start.18 = (f32[8,128,128]{2,1,0:T(8,128)S(1)}, f32[8,128,128]{2,1,0:T(8,128)}, u32[]{:S(2)}) copy-start(f32[8,128,128]{2,1,0:T(8,128)} %param.6) | copy-start | bytes 1572868
  37.6 10.5 %copy-start.19 = (f32[2,128,128]{2,1,0:T(8,128)S(1)}, f32[2,128,128]{2,1,0:T(8,128)}, u32[]{:S(2)}) copy-start(f32[2,128,128]{2,1,0:T(8,128)} %param.8) | copy-start | bytes 393220
  37.6 80.6 %all-to-all-start.1 = ((f32[32,2,128,128]{3,2,1,0:T(8,128)}), f32[32,2,128,128]{3,2,1,0:T(8,128)}, u32[]{:S(2)}, u32[]{:S(2)}) async-start(f32[32,2,128,128]{3,2,1,0:T(8,128)} %broadcast_select_fusion), calls=%async_computation.1 | async-start | bytes 8388608 | tf_op jit(solution)/shard_map/all_to_all | solution.py:180
  46.1 235.5 %reduce-scatter.3.cloned.1.call-start = ((), (), s32[]{:S(2)}) async-start(), calls=%async_computation.5 | async-start | bytes 1310720 | tf_op jit(solution)/shard_map/reduce_scatter | solution.py:137
  46.1 3.8 collective-permute-start
  152.7 1.2 copy-start.9
  152.7 1.5 copy-start.10
  154.3 1.2 copy-start.5
  154.3 1.5 copy-start.6
  155.8 1.2 copy-start.1
  155.8 1.5 copy-start.2
  157.3 0.7 copy-start.24
  158.0 6.4 %copy-start.21 = (s32[16,128]{1,0:T(8,128)S(1)}, s32[16,128]{1,0:T(8,128)}, u32[]{:S(2)}) copy-start(s32[16,128]{1,0:T(8,128)} %get-tuple-element.143) | copy-start | bytes 24580
  189.1 56.1 %collective-permute-start.1 = (f32[4,2,256,128]{2,3,1,0:T(8,128)S(1)}, f32[4,2,256,128]{2,3,1,0:T(8,128)S(1)}, u32[]{:S(2)}, u32[]{:S(2)}) collective-permute-start(f32[4,2,256,128]{2,3,1,0:T(8,128)S(1)} %slice.481), channel_id=1, source_target_pairs={{0,4},{4,8},{8,12},{12,16},{16,20},{20,24},{24,28},{28,32},{32,36}... | collective-permute-start | bytes 3145736 | tf_op jit(solution)/shard_map/ppermute | solution.py:15
  246.4 241.6 %reduce-scatter.5.cloned.1.call-start = ((), (), s32[]{:S(2)}) async-start(), calls=%async_computation.6 | async-start | bytes 1310720 | tf_op jit(solution)/shard_map/reduce_scatter | solution.py:137
  247.5 47.2 %copy-start.11 = (f32[1,2,256,128]{2,3,1,0:T(8,128)}, f32[1,2,256,128]{2,3,1,0:T(8,128)S(1)}, u32[]{:S(2)}) copy-start(f32[1,2,256,128]{2,3,1,0:T(8,128)S(1)} %copy.236) | copy-start | bytes 786436
  293.5 3.8 collective-permute-start.2
  368.7 3.6 copy-start.15
  368.7 3.6 copy-start.16
  372.3 3.3 copy-start.23
  375.6 3.1 copy-start.13
  375.6 3.1 copy-start.14
  406.6 1.2 copy-start.7
  406.6 1.5 copy-start.8
  408.1 1.2 copy-start.3
  408.1 1.5 copy-start.4
  409.7 1.2 copy-start
  411.1 6.4 %copy-start.22 = (s32[16,128]{1,0:T(8,128)S(1)}, s32[16,128]{1,0:T(8,128)}, u32[]{:S(2)}) copy-start(s32[16,128]{1,0:T(8,128)} %get-tuple-element.143) | copy-start | bytes 24580
  442.3 45.7 %copy-start.12 = (f32[1,2,256,128]{2,3,1,0:T(8,128)S(1)}, f32[1,2,256,128]{2,3,1,0:T(8,128)}, u32[]{:S(2)}) copy-start(f32[1,2,256,128]{2,3,1,0:T(8,128)} %copy-done.11) | copy-start | bytes 786436
  442.3 45.7 %copy-start.17 = (f32[1,2,256,128]{2,3,1,0:T(8,128)S(1)}, f32[1,2,256,128]{2,3,1,0:T(8,128)}, u32[]{:S(2)}) copy-start(f32[1,2,256,128]{2,3,1,0:T(8,128)} %reduce-scatter.3.cloned.1.call-done) | copy-start | bytes 786436
  442.3 10.9 %collective-permute-start.3 = (f32[4,2,256,128]{2,3,1,0:T(8,128)S(1)}, f32[4,2,256,128]{2,3,1,0:T(8,128)S(1)}, u32[]{:S(2)}, u32[]{:S(2)}) collective-permute-start(f32[4,2,256,128]{2,3,1,0:T(8,128)S(1)} %slice.507), channel_id=1, source_target_pairs={{0,4},{4,8},{8,12},{12,16},{16,20},{20,24},{24,28},{28,32},{32,36}... | collective-permute-start | bytes 3145736 | tf_op jit(solution)/shard_map/ppermute | solution.py:15
Sparse Core Ops, SparseCore 0:
  246.5 35.0 reduce-scatter.2
  454.5 33.4 reduce-scatter.4
